TPU v7x, 32 devices: a whole 2x2x4 slice. The times are simulated.
32 devices in a mesh: hop: 4 (over z), node: 8 (over y, x, core).
Axes of the slice: x: 2, y: 2, z: 4, core: 2. Of those that a mesh axis runs over, the one named last changes fastest.
Arguments:
- child_features: bfloat16 [16384, 1024], P(('hop', 'node')), may hold values from -6 to 6
- child_type: int32 [16384], P(('hop', 'node')), may hold values 0 or 1
- parent_features: bfloat16 [16384, 1024], P(('hop', 'node')), may hold values from -6 to 6
- child_slot: int32 [32, 32, 32], P(('hop', 'node')), may hold values from 0 to 511
- parent_slot: int32 [32, 32, 32], P(('hop', 'node')), may hold values from 0 to 511
- importance: int32 [32, 32, 32], P(('hop', 'node')), may hold values from 0 to 16, as said below
- board_proj: bfloat16 [512, 1024], replicated, may hold values from -0.25 to 0.25
- board_bias: float32 [1024], replicated, may hold values from -3 to 3
- neigh_weight: bfloat16 [1024, 1024], replicated, may hold values from -0.1875 to 0.1875
- neigh_bias: float32 [1024], replicated, may hold values from -3 to 3
- comb_weight: bfloat16 [2048, 1024], replicated, may hold values from -0.125 to 0.125
- comb_bias: float32 [1024], replicated, may hold values from -3 to 3
- out_grad: bfloat16 [16384, 1024], P(('hop', 'node')), may hold values from -6 to 6
Outputs:
- embedding: bfloat16 [16384, 1024], P(('hop', 'node'))
- child_grad: bfloat16 [16384, 1024], P(('hop', 'node'))
- parent_grad: bfloat16 [16384, 1024], P(('hop', 'node'))
- board_proj_grad: float32 [512, 1024], replicated
- board_bias_grad: float32 [1024], replicated
- neigh_weight_grad: float32 [1024, 1024], replicated
- neigh_bias_grad: float32 [1024], replicated
- comb_weight_grad: float32 [2048, 1024], replicated
- comb_bias_grad: float32 [1024], replicated
Inputs may be any that keep to these rules, and one draw needn't show every extreme that they name: For receiver r and sender s, importance[r, s, k] is positive for k below a count c(r, s) and 0 from there on; c(r, s) <= 32, and in every draw one receiver has c = 32 from every sender.
All inputs are finite; a program needn't handle non-finite values. No bound on the sum of `child_type` on one device may be relied on, other than what follows from the above.
Results may differ from a plain program's by a relative error of at most 0.0069.
Values may be sent and summed in bfloat16 or wider, within the bound.
A program may use at most 128 MiB of HBM per device.

v0:
```python
import jax
import jax.numpy as jnp
from jax import lax
from jax.sharding import PartitionSpec as P

epsilon = 1e-06


def outer_sum(left, right):
    return lax.dot_general(
        left, right, (((0,), (0,)), ((), ())), preferred_element_type=jnp.float32
    )


def times_transposed(left, right):
    return lax.dot_general(
        left, right, (((1,), (1,)), ((), ())), preferred_element_type=jnp.float32
    )


def silu_slope(value):
    sigma = jax.nn.sigmoid(value)
    return sigma * (1.0 + value * (1.0 - sigma))


def send_rows(buffer):
    return lax.all_to_all(buffer, ("hop", "node"), split_axis=0, concat_axis=0, tiled=True)


def send_grads(buffer):
    return lax.all_to_all(buffer, ("hop", "node"), split_axis=0, concat_axis=0, tiled=True)


def sum_gradients(parts):
    return lax.psum((parts[0], parts[1], parts[2], parts[3], parts[4], parts[5]), ("hop", "node"))


def body(
    child_features,
    child_type,
    parent_features,
    child_slot,
    parent_slot,
    importance,
    board_proj,
    board_bias,
    neigh_weight,
    neigh_bias,
    comb_weight,
    comb_bias,
    out_grad,
):
    width_board = board_proj.shape[0]
    feat_width = child_features.shape[1]
    child_count = child_features.shape[0]
    parent_count = parent_features.shape[0]
    hidden_width = neigh_weight.shape[1]
    senders = child_slot.shape[1]
    capacity = child_slot.shape[2]
    board = (child_type == 1)[:, None]
    left_part = child_features[:, :width_board]
    board_pre = jnp.dot(left_part, board_proj, preferred_element_type=jnp.float32) + board_bias
    child_in = jnp.where(board, board_pre.astype(jnp.bfloat16), child_features)
    neigh_pre = jnp.dot(child_in, neigh_weight, preferred_element_type=jnp.float32) + neigh_bias
    neigh = jax.nn.silu(neigh_pre).astype(jnp.bfloat16)
    child_rows = child_slot.reshape(-1)
    outgoing = jnp.take(neigh, child_rows, axis=0).reshape(senders, capacity, hidden_width)
    incoming = send_rows(outgoing).reshape(senders * capacity, hidden_width)
    weights = importance.reshape(-1).astype(jnp.float32)
    targets = parent_slot.reshape(-1)
    matches = targets[None, :] == jnp.arange(parent_count, dtype=jnp.int32)[:, None]
    weighted = jnp.where(matches, weights[None, :], 0.0)
    total = jnp.maximum(jnp.sum(weighted, axis=1), 1.0)
    sums = jnp.dot(weighted.astype(jnp.bfloat16), incoming, preferred_element_type=jnp.float32)
    agg = sums / total[:, None]
    cat = jnp.concatenate([parent_features, agg.astype(jnp.bfloat16)], axis=1)
    comb_pre = jnp.dot(cat, comb_weight, preferred_element_type=jnp.float32) + comb_bias
    hidden_z = jax.nn.silu(comb_pre)
    inverse = lax.rsqrt(jnp.sum(hidden_z * hidden_z, axis=1, keepdims=True) + epsilon)
    normed = hidden_z * inverse
    embedding = normed.astype(jnp.bfloat16)
    grad_y = out_grad.astype(jnp.float32)
    grad_z = inverse * (grad_y - normed * jnp.sum(normed * grad_y, axis=1, keepdims=True))
    grad_comb = (grad_z * silu_slope(comb_pre)).astype(jnp.bfloat16)
    comb_weight_grad = outer_sum(cat, grad_comb)
    comb_bias_grad = jnp.sum(grad_comb.astype(jnp.float32), axis=0)
    grad_cat = times_transposed(grad_comb, comb_weight)
    parent_grad = grad_cat[:, :feat_width].astype(jnp.bfloat16)
    grad_scaled = grad_cat[:, feat_width:] / total[:, None]
    grad_edges = (jnp.take(grad_scaled, targets, axis=0) * weights[:, None]).astype(jnp.bfloat16)
    returned = send_grads(grad_edges.reshape(senders, capacity, hidden_width))
    grad_neigh = jax.ops.segment_sum(
        returned.reshape(senders * capacity, hidden_width).astype(jnp.float32),
        child_rows,
        num_segments=child_count,
    )
    grad_npre = (grad_neigh * silu_slope(neigh_pre)).astype(jnp.bfloat16)
    neigh_weight_grad = outer_sum(child_in, grad_npre)
    neigh_bias_grad = jnp.sum(grad_npre.astype(jnp.float32), axis=0)
    grad_in = times_transposed(grad_npre, neigh_weight)
    grad_board = jnp.where(board, grad_in, 0.0).astype(jnp.bfloat16)
    board_proj_grad = outer_sum(left_part, grad_board)
    board_bias_grad = jnp.sum(grad_board.astype(jnp.float32), axis=0)
    grad_left = times_transposed(grad_board, board_proj)
    padding = jnp.zeros((child_count, feat_width - width_board), jnp.float32)
    board_rows = jnp.concatenate([grad_left, padding], axis=1)
    child_grad = jnp.where(board, board_rows, grad_in).astype(jnp.bfloat16)
    summed = sum_gradients(
        (
            board_proj_grad,
            board_bias_grad,
            neigh_weight_grad,
            neigh_bias_grad,
            comb_weight_grad,
            comb_bias_grad,
        )
    )
    return (
        embedding,
        child_grad,
        parent_grad,
        summed[0],
        summed[1],
        summed[2],
        summed[3],
        summed[4],
        summed[5],
    )


def solution(mesh):
    in_specs = (
        P(("hop", "node"), None),
        P(("hop", "node")),
        P(("hop", "node"), None),
        P(("hop", "node"), None, None),
        P(("hop", "node"), None, None),
        P(("hop", "node"), None, None),
        P(),
        P(),
        P(),
        P(),
        P(),
        P(),
        P(("hop", "node"), None),
    )
    out_specs = (
        P(("hop", "node"), None),
        P(("hop", "node"), None),
        P(("hop", "node"), None),
        P(),
        P(),
        P(),
        P(),
        P(),
        P(),
    )
    return jax.shard_map(body, mesh=mesh, in_specs=in_specs, out_specs=out_specs, check_vma=False)
```

profile of v0, /device:TPU:0, one launch (start us, length us, event | category | flops | bytes accessed | tf_op | source)
XLA Modules:
  0.0 455.3 jit_solution(8756432768272491844)
XLA Ops:
  9.6 2.4 fusion.7
  12.1 2.7 multiply_convert_fusion.2
  14.8 5.3 %gather_fusion = bf16[1024,1024]{1,0:T(8,128)(2,1)} fusion(bf16[512,1024]{1,0:T(8,128)(2,1)S(1)} %get-tuple-element.33, s32[1024]{0:T(1024)S(1)} %broadcast_clamp_fusion.1), kind=kCustom, calls=%fused_computation | custom fusion | bytes 4198400 | tf_op jit(solution)/shard_map/jit(_take)/gather | solution.py:67
  20.1 3.2 broadcast_select_fusion
  23.3 7.4 %all-to-all-start = ((bf16[32,32,1024]{2,1,0:T(8,128)(2,1)}), bf16[32,32,1024]{2,1,0:T(8,128)(2,1)}, u32[]{:S(2)}, u32[]{:S(2)}) async-start(bf16[32,32,1024]{2,1,0:T(8,128)(2,1)} %broadcast_select_fusion), calls=%async_computation | async-start | bytes 4194304 | tf_op jit(solution)/shard_map/all_to_all | solution.py:27
  31.3 48.3 %all-to-all-done = bf16[32,32,1024]{2,1,0:T(8,128)(2,1)} async-done(((bf16[32,32,1024]{2,1,0:T(8,128)(2,1)}), bf16[32,32,1024]{2,1,0:T(8,128)(2,1)}, u32[]{:S(2)}, u32[]{:S(2)}) %all-to-all-start) | async-done | bytes 2097184 | tf_op jit(solution)/shard_map/all_to_all | solution.py:27
  79.6 3.0 divide_convert_fusion
  82.8 2.8 multiply_reduce_fusion
  88.6 2.4 fusion.20
  94.5 7.9 %gather_fusion.1 = f32[1024,1024]{1,0:T(8,128)} fusion(f32[512,1024]{1,0:T(8,128)} %slice_divide_fusion, s32[1024]{0:T(1024)S(1)} %broadcast_clamp_fusion), kind=kCustom, calls=%fused_computation.1 | custom fusion | bytes 8392704 | tf_op jit(solution)/shard_map/jit(_take)/gather | solution.py:90
  102.4 3.9 multiply_convert_fusion
  106.4 4.1 all-to-all-start.1
  110.6 7.3 %fusion.8 = f32[2048,1024]{1,0:T(8,128)} fusion(bf16[512,1024]{1,0:T(8,128)(2,1)S(1)} %get-tuple-element.25, bf16[512,1024]{1,0:T(8,128)(2,1)} %copy-done.15, bf16[512,1024]{1,0:T(8,128)(2,1)} %param.15), kind=kOutput, calls=%fused_computation.35 | convolution fusion | flops 2151677952 | bytes 11534336 | tf_op jit(solution)/shard_map/dot_general | solution.py:10
  118.0 41.4 %all-to-all-done.1 = bf16[32,32,1024]{2,1,0:T(8,128)(2,1)} async-done(((bf16[32,32,1024]{2,1,0:T(8,128)(2,1)}), bf16[32,32,1024]{2,1,0:T(8,128)(2,1)}, u32[]{:S(2)}, u32[]{:S(2)}) %all-to-all-start.1) | async-done | bytes 2097184 | tf_op jit(solution)/shard_map/all_to_all | solution.py:31
  159.4 11.1 %scatter_custom_fusion = f32[512,1024]{1,0:T(8,128)} fusion(s32[1024]{0:T(1024)S(1)} %reshape.170, bf16[1024,1024]{1,0:T(8,128)(2,1)} %bitcast.10, f32[]{:T(128)} %constant.21.clone.1), kind=kCustom, calls=%fused_computation.3 | custom fusion | flops 2097152 | bytes 4194308 | tf_op jit(solution)/shard_map/scatter-add | solution.py:92
  170.5 3.1 convert_reduce_fusion.1
  173.5 2.3 convert_reduce_fusion.2
  175.8 3.3 fusion.22
  181.2 2.7 slice.25
  183.9 40.1 %all-reduce.1 = (f32[1024]{0:T(1024)}, f32[1024]{0:T(1024)}, f32[1024]{0:T(1024)}) all-reduce(f32[1024]{0:T(1024)S(1)} %get-tuple-element.28, f32[1024]{0:T(1024)S(1)} %get-tuple-element.26, f32[1024]{0:T(1024)S(1)} %get-tuple-element.24), channel_id=1, replica_groups=mesh['hop'=4,'node'=8] {'hop','node'}, use_global_device_ids=true, to_apply=%region_6.7 | all-reduce | flops 3072 | bytes 24576 | tf_op jit(solution)/shard_map/psum | solution.py:35
  227.4 208.7 %all-reduce.5.cloned.1.call-done = (f32[512,1024]{0,1:T(8,128)}, f32[1024,1024]{1,0:T(8,128)}, f32[2048,1024]{1,0:T(8,128)}) async-done(((f32[512,1024]{0,1:T(8,128)}, f32[1024,1024]{1,0:T(8,128)}, f32[2048,1024]{1,0:T(8,128)}), (f32[512,1024]{0,1:T(8,128)}, f32[1024,1024]{1,0:T(8,128)}, f32[2048,1024]{1,0:T(8,128)})) %all-reduce.5.cloned.1.call-update) | async-done | bytes 14680080 | tf_op jit(solution)/shard_map/psum | solution.py:35
  436.1 2.9 copy.22
  439.0 5.1 %copy.26 = f32[1024,1024]{1,0:T(8,128)} copy(f32[1024,1024]{1,0:T(8,128)} %get-tuple-element.43) | data formatting | bytes 8388608
  445.1 3.4 copy.27
  (56 shorter events, 16.3 us)
Async XLA Ops:
  7.2 4.8 %copy-start = (bf16[1024,1024]{1,0:T(8,128)(2,1)S(1)}, bf16[1024,1024]{1,0:T(8,128)(2,1)}, u32[]{:S(2)}) copy-start(bf16[1024,1024]{1,0:T(8,128)(2,1)} %param.21) | copy-start | bytes 6291460
  9.6 2.5 copy-start.12
  12.0 2.8 copy-start.4
  23.3 7.4 %copy-start.8 = (s32[1,32,32]{2,1,0:T(8,128)S(1)}, s32[1,32,32]{2,1,0:T(8,128)}, u32[]{:S(2)}) copy-start(s32[1,32,32]{2,1,0:T(8,128)} %param.17) | copy-start | bytes 12292
  23.3 7.6 %copy-start.10 = (s32[1,32,32]{2,1,0:T(8,128)S(1)}, s32[1,32,32]{2,1,0:T(8,128)}, u32[]{:S(2)}) copy-start(s32[1,32,32]{2,1,0:T(8,128)} %param.18) | copy-start | bytes 12292
  23.3 56.3 %all-to-all-start = ((bf16[32,32,1024]{2,1,0:T(8,128)(2,1)}), bf16[32,32,1024]{2,1,0:T(8,128)(2,1)}, u32[]{:S(2)}, u32[]{:S(2)}) async-start(bf16[32,32,1024]{2,1,0:T(8,128)(2,1)} %broadcast_select_fusion), calls=%async_computation | async-start | bytes 4194304 | tf_op jit(solution)/shard_map/all_to_all | solution.py:27
  79.6 3.0 copy-start.11
  79.6 3.0 copy-start.13
  79.6 3.1 copy-start.14
  82.8 2.8 copy-start.15
  82.8 2.8 copy-start.2
  91.0 2.0 copy-start.3
  106.4 4.2 copy-start.9
  106.4 53.0 %all-to-all-start.1 = ((bf16[32,32,1024]{2,1,0:T(8,128)(2,1)}), bf16[32,32,1024]{2,1,0:T(8,128)(2,1)}, u32[]{:S(2)}, u32[]{:S(2)}) async-start(bf16[32,32,1024]{2,1,0:T(8,128)(2,1)} %multiply_convert_fusion), calls=%async_computation.1 | async-start | bytes 4194304 | tf_op jit(solution)/shard_map/all_to_all | solution.py:31
  110.5 325.6 %all-reduce.5.cloned.1.call-start = ((), (), s32[]{:S(2)}) async-start(), calls=%async_computation.2 | async-start | bytes 29360128 | tf_op jit(solution)/shard_map/psum | solution.py:35
  173.5 2.3 copy-start.5
  175.8 3.3 copy-start.7
  224.0 2.1 copy-start.6
  438.9 6.2 %copy-start.1 = (f32[2048,1024]{1,0:T(8,128)S(1)}, f32[2048,1024]{1,0:T(8,128)}, u32[]{:S(2)}) copy-start(f32[2048,1024]{1,0:T(8,128)} %get-tuple-element.45) | copy-start | bytes 25165828
Sparse Core Ops, SparseCore 0:
  181.3 254.6 all-reduce.4
where the time goes:
time: 456 us; the launch traced here: 455 us
  waiting for transfers between devices  298 us (65%)
  blocking collectives  40.1 us (9%)
  local copies, waits for them, and re-layouts  31.8 us (7%)
  matrix products  30.4 us (7%)
  other arithmetic  28.9 us (6%)
  between operations  14.3 us (3%)
  starting transfers between devices  11.6 us (3%)
    psum x1, waiting for transfers between devices, sum_gradients(): lax.psum((parts[0], parts[1], parts[2], parts[3], parts[4], parts[5]), ('...  209 us
    all_to_all x1, waiting for transfers between devices, send_rows(): lax.all_to_all(buffer, ('hop', 'node'), split_axis=0, concat_axis=0, tile...  48.3 us
    all_to_all x1, waiting for transfers between devices, send_grads(): lax.all_to_all(buffer, ('hop', 'node'), split_axis=0, concat_axis=0, tile...  41.4 us
    psum x1, blocking collectives, sum_gradients(): lax.psum((parts[0], parts[1], parts[2], parts[3], parts[4], parts[5]), ('...  40.1 us
    unnamed x35, local copies, waits for them, and re-layouts  14.6 us
    dot_general x3, matrix products, outer_sum(): lax.dot_general(left, right, (((0,), (0,)), ((), ())), preferred_element_...  12.7 us
    scatter-add x1, other arithmetic, body(): jax.ops.segment_sum(returned.reshape(senders * capacity, hidden_width).as...  11.1 us
  transfers between devices with their start and end apart: 3, of which 3 were waited for; matrix products, arithmetic and copies ran while one was open for 3% of the time, Pallas kernels for 0%

commit v1 on v0

--- a/solution.py
+++ b/solution.py
@@ -32,7 +32,9 @@
 
 
 def sum_gradients(parts):
-    return lax.psum((parts[0], parts[1], parts[2], parts[3], parts[4], parts[5]), ("hop", "node"))
+    return lax.psum(
+        lax.psum((parts[0], parts[1], parts[2], parts[3], parts[4], parts[5]), "node"), "hop"
+    )
 
 
 def body(

time: 456 us -> 896 us (1.96)
  waiting for transfers between devices: 298 us -> 734 us
    psum x1 -> x2, waiting for transfers between devices: 209 us -> 644 us  [the longest x1 448 us: sum_gradients(): lax.psum(lax.psum((parts[0], parts[1], parts[2], parts[3], parts[4], part...]
    psum x1 -> x2, blocking collectives: 40.1 us -> 44.4 us  [the longest x1 24.5 us: sum_gradients(): lax.psum((parts[0], parts[1], parts[2], parts[3], parts[4], parts[5]), 'n...]
  transfers between devices with their start and end apart: 3 -> 4, of which waited for: 3 -> 4; matrix products, arithmetic and copies ran while one was open for 3% -> 2% of each run, Pallas kernels for 0% -> 0%
where the time goes in v1:
time: 896 us; the launch traced here: 895 us
  waiting for transfers between devices  734 us (82%)
  blocking collectives  44.4 us (5%)
  local copies, waits for them, and re-layouts  31.8 us (4%)
  matrix products  30.3 us (3%)
  other arithmetic  28.9 us (3%)
  between operations  14.3 us (2%)
  starting transfers between devices  11.6 us (1%)
    psum x1, waiting for transfers between devices, sum_gradients(): lax.psum(lax.psum((parts[0], parts[1], parts[2], parts[3], parts[4], part...  448 us
    psum x1, waiting for transfers between devices, sum_gradients(): lax.psum((parts[0], parts[1], parts[2], parts[3], parts[4], parts[5]), 'n...  195 us
    all_to_all x1, waiting for transfers between devices, send_rows(): lax.all_to_all(buffer, ('hop', 'node'), split_axis=0, concat_axis=0, tile...  48.3 us
    all_to_all x1, waiting for transfers between devices, send_grads(): lax.all_to_all(buffer, ('hop', 'node'), split_axis=0, concat_axis=0, tile...  41.4 us
    psum x1, blocking collectives, sum_gradients(): lax.psum((parts[0], parts[1], parts[2], parts[3], parts[4], parts[5]), 'n...  24.5 us
    psum x1, blocking collectives, sum_gradients(): lax.psum(lax.psum((parts[0], parts[1], parts[2], parts[3], parts[4], part...  19.9 us
  transfers between devices with their start and end apart: 4, of which 4 were waited for; matrix products, arithmetic and copies ran while one was open for 2% of the time, Pallas kernels for 0%

profile of v1, /device:TPU:0, one launch (start us, length us, event | category | flops | bytes accessed | tf_op | source)
XLA Modules:
  0.0 894.8 jit_solution(5540197482688980256)
XLA Ops:
  9.6 2.4 fusion.7
  12.1 2.7 multiply_convert_fusion.2
  14.8 5.3 gather_fusion
  20.1 3.2 broadcast_select_fusion
  23.3 7.4 all-to-all-start
  31.3 48.3 %all-to-all-done = bf16[32,32,1024]{2,1,0:T(8,128)(2,1)} async-done(((bf16[32,32,1024]{2,1,0:T(8,128)(2,1)}), bf16[32,32,1024]{2,1,0:T(8,128)(2,1)}, u32[]{:S(2)}, u32[]{:S(2)}) %all-to-all-start) | async-done | bytes 2097184 | tf_op jit(solution)/shard_map/all_to_all | solution.py:27
  79.6 3.0 divide_convert_fusion
  82.8 2.8 multiply_reduce_fusion
  94.5 7.9 gather_fusion.1
  102.4 3.9 multiply_convert_fusion
  106.4 4.1 all-to-all-start.1
  110.6 7.3 fusion.8
  117.9 41.4 %all-to-all-done.1 = bf16[32,32,1024]{2,1,0:T(8,128)(2,1)} async-done(((bf16[32,32,1024]{2,1,0:T(8,128)(2,1)}), bf16[32,32,1024]{2,1,0:T(8,128)(2,1)}, u32[]{:S(2)}, u32[]{:S(2)}) %all-to-all-start.1) | async-done | bytes 2097184 | tf_op jit(solution)/shard_map/all_to_all | solution.py:31
  159.4 11.1 %scatter_custom_fusion = f32[512,1024]{1,0:T(8,128)} fusion(s32[1024]{0:T(1024)S(1)} %reshape.170, bf16[1024,1024]{1,0:T(8,128)(2,1)} %bitcast.10, f32[]{:T(128)} %constant.21.clone.1), kind=kCustom, calls=%fused_computation.3 | custom fusion | flops 2097152 | bytes 4194308 | tf_op jit(solution)/shard_map/scatter-add | solution.py:94
  170.4 3.1 convert_reduce_fusion.1
  175.8 3.3 fusion.22
  181.2 195.5 %all-reduce.8.cloned.1.call-done = (f32[512,1024]{0,1:T(8,128)}, f32[1024,1024]{1,0:T(8,128)}, f32[2048,1024]{1,0:T(8,128)}) async-done(((f32[512,1024]{0,1:T(8,128)}, f32[1024,1024]{1,0:T(8,128)}, f32[2048,1024]{1,0:T(8,128)}), (f32[512,1024]{0,1:T(8,128)}, f32[1024,1024]{1,0:T(8,128)}, f32[2048,1024]{1,0:T(8,128)})) %all-reduce.8.cloned.1.call-update) | async-done | bytes 14680080 | tf_op jit(solution)/shard_map/psum | solution.py:36
  376.7 2.7 slice.25
  379.5 24.5 %all-reduce.1 = (f32[1024]{0:T(1024)S(1)}, f32[1024]{0:T(1024)S(1)}, f32[1024]{0:T(1024)S(1)}) all-reduce(f32[1024]{0:T(1024)S(1)} %get-tuple-element.34, f32[1024]{0:T(1024)S(1)} %get-tuple-element.32, f32[1024]{0:T(1024)S(1)} %get-tuple-element.30), channel_id=1, replica_groups=mesh['hop'=4,'node'=8] {'node'}, use_global_device_ids=true, to_apply=%region_7.8 | all-reduce | flops 3072 | bytes 24576 | tf_op jit(solution)/shard_map/psum | solution.py:36
  404.0 19.9 %all-reduce.3 = (f32[1024]{0:T(1024)}, f32[1024]{0:T(1024)}, f32[1024]{0:T(1024)}) all-reduce(f32[1024]{0:T(1024)S(1)} %get-tuple-element.18, f32[1024]{0:T(1024)S(1)} %get-tuple-element.19, f32[1024]{0:T(1024)S(1)} %get-tuple-element.20), channel_id=1, replica_groups=mesh['hop'=4,'node'=8] {'hop'}, use_global_device_ids=true, to_apply=%region_8.9 | all-reduce | flops 3072 | bytes 24576 | tf_op jit(solution)/shard_map/psum | solution.py:35
  427.2 448.4 %all-reduce.10.cloned.1.call-done = (f32[512,1024]{0,1:T(8,128)}, f32[1024,1024]{1,0:T(8,128)}, f32[2048,1024]{1,0:T(8,128)}) async-done(((f32[512,1024]{0,1:T(8,128)}, f32[1024,1024]{1,0:T(8,128)}, f32[2048,1024]{1,0:T(8,128)}), (f32[512,1024]{0,1:T(8,128)}, f32[1024,1024]{1,0:T(8,128)}, f32[2048,1024]{1,0:T(8,128)})) %all-reduce.10.cloned.1.call-update) | async-done | bytes 14680080 | tf_op jit(solution)/shard_map/psum | solution.py:35
  875.5 2.9 copy.22
  878.4 5.1 copy.29
  884.6 3.4 copy.30
  (60 shorter events, 20.9 us)
Async XLA Ops:
  7.2 4.8 copy-start
  9.6 2.5 copy-start.12
  12.0 2.8 copy-start.4
  23.3 7.4 copy-start.8
  23.3 7.6 copy-start.10
  23.3 56.3 %all-to-all-start = ((bf16[32,32,1024]{2,1,0:T(8,128)(2,1)}), bf16[32,32,1024]{2,1,0:T(8,128)(2,1)}, u32[]{:S(2)}, u32[]{:S(2)}) async-start(bf16[32,32,1024]{2,1,0:T(8,128)(2,1)} %broadcast_select_fusion), calls=%async_computation | async-start | bytes 4194304 | tf_op jit(solution)/shard_map/all_to_all | solution.py:27
  79.6 3.0 copy-start.11
  79.6 3.0 copy-start.13
  79.6 3.1 copy-start.14
  82.8 2.8 copy-start.15
  82.8 2.8 copy-start.2
  91.0 1.9 copy-start.3
  106.4 4.2 copy-start.9
  106.4 53.0 %all-to-all-start.1 = ((bf16[32,32,1024]{2,1,0:T(8,128)(2,1)}), bf16[32,32,1024]{2,1,0:T(8,128)(2,1)}, u32[]{:S(2)}, u32[]{:S(2)}) async-start(bf16[32,32,1024]{2,1,0:T(8,128)(2,1)} %multiply_convert_fusion), calls=%async_computation.1 | async-start | bytes 4194304 | tf_op jit(solution)/shard_map/all_to_all | solution.py:31
  110.5 266.2 %all-reduce.8.cloned.1.call-start = ((), (), s32[]{:S(2)}) async-start(), calls=%async_computation.2 | async-start | bytes 29360128 | tf_op jit(solution)/shard_map/psum | solution.py:36
  173.5 2.3 copy-start.5
  175.8 3.3 copy-start.7
  181.2 694.3 %all-reduce.10.cloned.1.call-start = ((), (), s32[]{:S(2)}) async-start(), calls=%async_computation.3 | async-start | bytes 29360128 | tf_op jit(solution)/shard_map/psum | solution.py:35
  423.8 2.1 copy-start.6
  878.4 6.2 copy-start.1
Sparse Core Ops, SparseCore 0:
  181.3 195.3 all-reduce.7
  379.8 495.7 all-reduce.9
